TPU v7x, 32 devices: a whole 2x2x4 slice. The times are simulated.
32 devices in a mesh: replica: 16 (over z, x, core), fsdp: 2 (over y).
Axes of the slice: x: 2, y: 2, z: 4, core: 2. Of those that a mesh axis runs over, the one named last changes fastest.
Arguments:
- block_in: bfloat16 [4096, 1024], P(('replica', 'fsdp')), may hold values from -6 to 6
- w_query: bfloat16 [1024, 2048], P('fsdp'), may hold values from -1 to 1
- key_projection: bfloat16 [1024, 1024], P('fsdp'), may hold values from -1 to 1
- value_projection: bfloat16 [1024, 1024], P('fsdp'), may hold values from -0.1875 to 0.1875
- w_out: bfloat16 [2048, 1024], P('fsdp'), may hold values from -0.5 to 0.5
- w_gate: bfloat16 [1024, 3072], P('fsdp'), may hold values from -0.1875 to 0.1875
- w_up: bfloat16 [1024, 3072], P('fsdp'), may hold values from -0.1875 to 0.1875
- w_down: bfloat16 [3072, 1024], P('fsdp'), may hold values from -0.109375 to 0.109375
- attn_gain: float32 [1024], replicated, may hold values from 0.5 to 1.5
- mlp_gain: float32 [1024], replicated, may hold values from 0.5 to 1.5
- query_gain: float32 [128], replicated, may hold values from 0.5 to 3.5
- key_norm_gain: float32 [128], replicated, may hold values from 0.5 to 3.5
- segment_ids: int32 [16, 256], P('replica'), may hold values from 0 to 2, as said below
- positions: int32 [4096], P(('replica', 'fsdp')), may hold values from 0 to 255, as said below
- cotangent: bfloat16 [4096, 1024], P(('replica', 'fsdp')), may hold values from -6 to 6
Outputs:
- block_out: bfloat16 [4096, 1024], P(('replica', 'fsdp'))
- d_block_in: float32 [4096, 1024], P(('replica', 'fsdp'))
- grad_query: float32 [1024, 2048], P('fsdp')
- grad_key: float32 [1024, 1024], P('fsdp')
- grad_value: float32 [1024, 1024], P('fsdp')
- grad_out: float32 [2048, 1024], P('fsdp')
- grad_gate: float32 [1024, 3072], P('fsdp')
- grad_up: float32 [1024, 3072], P('fsdp')
- grad_down: float32 [3072, 1024], P('fsdp')
- grad_attn_gain: float32 [1024], replicated
- grad_mlp_gain: float32 [1024], replicated
- grad_query_gain: float32 [128], replicated
- grad_key_gain: float32 [128], replicated
Inputs may be any that keep to these rules, and one draw needn't show every extreme that they name: `segment_ids`: in each sequence the document numbers start at 0 at its first token and rise by one at each new document, never falling; a sequence holds at most three documents, the first sequence a single one, every other sequence exactly three. `positions`: A token's position is its place within its document, counted from 0 at the document's first token.
All inputs are finite; a program needn't handle non-finite values.
Results may differ from a plain program's by a relative error of at most 0.02.
The roundings to bfloat16 on the way count: a program that leaves them out, or rounds other values in their place, can miss the bound.
Values may be sent and summed in bfloat16 or wider, within the bound.
No kernel may reach another device: no remote copies, remote signals or barrier semaphores. Data moves between devices by JAX's collectives and lax.ppermute only.
A program may use at most 192 MiB of HBM per device.

v0:
```python
import jax
import jax.numpy as jnp
from jax import lax
from jax.sharding import PartitionSpec as P

QUERY_HEADS = 16
KEY_VALUE_HEADS = 8
HEAD_SIZE = 128
EPS = 1e-06
THETA = 1000000.0
NEG = -1e30


def inv_rms(value):
    return lax.rsqrt(jnp.mean(value * value, axis=-1, keepdims=True) + EPS)


def norm_backward(grad, value, scale, gain):
    upstream = grad * gain
    return scale * (
        upstream - value * scale * scale * jnp.mean(upstream * value, axis=-1, keepdims=True)
    )


def rope_tables(position_row, width):
    half = width // 2
    freq = jnp.exp(
        -(jnp.arange(half, dtype=jnp.float32) * (2.0 / width)) * jnp.log(jnp.float32(THETA))
    )
    angle = position_row.astype(jnp.float32)[:, None] * freq[None, :]
    cos_tab = jnp.concatenate([jnp.cos(angle), jnp.cos(angle)], axis=-1)[:, None, :]
    sin_tab = jnp.concatenate([jnp.sin(angle), jnp.sin(angle)], axis=-1)[:, None, :]
    return (cos_tab, sin_tab)


def rotate(values_in):
    half = values_in.shape[-1] // 2
    return jnp.concatenate([-values_in[..., half:], values_in[..., :half]], axis=-1)


def rotate_back(values_in):
    half = values_in.shape[-1] // 2
    return jnp.concatenate([values_in[..., half:], -values_in[..., :half]], axis=-1)


def plain_product(left, right):
    return jnp.dot(left, right, preferred_element_type=jnp.float32)


def dot_right_t(left, right):
    return lax.dot_general(
        left, right, (((1,), (1,)), ((), ())), preferred_element_type=jnp.float32
    )


def rounded_partial(left, right):
    return lax.dot_general(
        left, right, (((0,), (0,)), ((), ())), preferred_element_type=jnp.bfloat16
    )


def attention_weights(w_query, key_projection, value_projection, w_out):
    return (
        lax.all_gather(w_query, "fsdp", axis=0, tiled=True),
        lax.all_gather(key_projection, "fsdp", axis=0, tiled=True),
        lax.all_gather(value_projection, "fsdp", axis=0, tiled=True),
        lax.all_gather(w_out, "fsdp", axis=0, tiled=True),
    )


def mlp_weights(w_gate, w_up, w_down):
    return (
        lax.all_gather(w_gate, "fsdp", axis=0, tiled=True),
        lax.all_gather(w_up, "fsdp", axis=0, tiled=True),
        lax.all_gather(w_down, "fsdp", axis=0, tiled=True),
    )


def context(k_rot, value_rows):
    return (
        lax.all_gather(k_rot, "fsdp", axis=0, tiled=True),
        lax.all_gather(value_rows, "fsdp", axis=0, tiled=True),
    )


def masked_scores(grouped_heads, keys_all, allowed):
    scores = jnp.einsum(
        "nkgd,mkd->kgnm", grouped_heads, keys_all, preferred_element_type=jnp.float32
    ) * HEAD_SIZE ** (-0.5)
    return jnp.where(allowed[None, None], scores, NEG)


def attend(query_rotated, keys_all, values_all, allowed):
    item_count = query_rotated.shape[0]
    grouped_heads = query_rotated.reshape(
        item_count, KEY_VALUE_HEADS, QUERY_HEADS // KEY_VALUE_HEADS, HEAD_SIZE
    )
    scores = masked_scores(grouped_heads, keys_all, allowed)
    top = jnp.max(scores, axis=-1, keepdims=True)
    lse = top + jnp.log(jnp.sum(jnp.exp(scores - top), axis=-1, keepdims=True))
    probs = jnp.exp(scores - lse).astype(jnp.bfloat16)
    mixed = jnp.einsum("kgnm,mkd->nkgd", probs, values_all, preferred_element_type=jnp.float32)
    return (mixed.astype(jnp.bfloat16).reshape(item_count, QUERY_HEADS * HEAD_SIZE), lse)


def attend_back(query_rotated, keys_all, values_all, allowed, lse, attention_gradient):
    item_count = query_rotated.shape[0]
    grouped_heads = query_rotated.reshape(
        item_count, KEY_VALUE_HEADS, QUERY_HEADS // KEY_VALUE_HEADS, HEAD_SIZE
    )
    grouped_gradient = attention_gradient.reshape(
        item_count, KEY_VALUE_HEADS, QUERY_HEADS // KEY_VALUE_HEADS, HEAD_SIZE
    )
    probs = jnp.exp(masked_scores(grouped_heads, keys_all, allowed) - lse)
    probs_b = probs.astype(jnp.bfloat16)
    d_prob = jnp.einsum(
        "nkgd,mkd->kgnm", grouped_gradient, values_all, preferred_element_type=jnp.float32
    )
    d_scores = (
        probs * (d_prob - jnp.sum(probs * d_prob, axis=-1, keepdims=True)) * HEAD_SIZE ** (-0.5)
    ).astype(jnp.bfloat16)
    d_qrot = jnp.einsum(
        "kgnm,mkd->nkgd", d_scores, keys_all, preferred_element_type=jnp.float32
    ).reshape(item_count, QUERY_HEADS, HEAD_SIZE)
    d_krot = jnp.einsum(
        "kgnm,nkgd->mkd", d_scores, grouped_heads, preferred_element_type=jnp.float32
    )
    values_gradient = jnp.einsum(
        "kgnm,nkgd->mkd", probs_b, grouped_gradient, preferred_element_type=jnp.float32
    )
    return (d_qrot, d_krot, values_gradient)


def shards(
    block_in,
    w_query,
    key_projection,
    value_projection,
    w_out,
    w_gate,
    w_up,
    w_down,
    attn_gain,
    mlp_gain,
    query_gain,
    key_norm_gain,
    segment_ids,
    positions,
    cotangent,
):
    item_count = block_in.shape[0]
    segment_row = segment_ids[0]
    sequence_length = segment_row.shape[0]
    offset = lax.axis_index("fsdp") * item_count
    local_segments = lax.dynamic_slice_in_dim(segment_row, offset, item_count)
    query_index = offset + jnp.arange(item_count, dtype=jnp.int32)
    key_index = jnp.arange(sequence_length, dtype=jnp.int32)
    allowed = (key_index[None, :] <= query_index[:, None]) & (
        segment_row[None, :] == local_segments[:, None]
    )
    resid = block_in.astype(jnp.float32)
    scale_one = inv_rms(resid)
    normed_rows = (resid * scale_one * attn_gain).astype(jnp.bfloat16)
    query_all, key_gathered, value_gathered, out_all = attention_weights(
        w_query, key_projection, value_projection, w_out
    )
    q_raw = plain_product(normed_rows, query_all).reshape(item_count, QUERY_HEADS, HEAD_SIZE)
    key_unnormed = plain_product(normed_rows, key_gathered).reshape(
        item_count, KEY_VALUE_HEADS, HEAD_SIZE
    )
    value_rows = (
        plain_product(normed_rows, value_gathered)
        .astype(jnp.bfloat16)
        .reshape(item_count, KEY_VALUE_HEADS, HEAD_SIZE)
    )
    q_scale = inv_rms(q_raw)
    key_scale = inv_rms(key_unnormed)
    q_normed = q_raw * q_scale * query_gain
    k_normed = key_unnormed * key_scale * key_norm_gain
    cos_tab, sin_tab = rope_tables(positions, HEAD_SIZE)
    query_rotated = (q_normed * cos_tab + rotate(q_normed) * sin_tab).astype(jnp.bfloat16)
    k_rot = (k_normed * cos_tab + rotate(k_normed) * sin_tab).astype(jnp.bfloat16)
    keys_all, values_all = context(k_rot, value_rows)
    attn_out, lse = attend(query_rotated, keys_all, values_all, allowed)
    mid = resid + plain_product(attn_out, out_all)
    scale_two = inv_rms(mid)
    normed_two = (mid * scale_two * mlp_gain).astype(jnp.bfloat16)
    gate_all, up_all, down_all = mlp_weights(w_gate, w_up, w_down)
    gate = plain_product(normed_two, gate_all)
    up = plain_product(normed_two, up_all)
    sig = jax.nn.sigmoid(gate)
    hidden = (gate * sig * up).astype(jnp.bfloat16)
    block_out = (mid + plain_product(hidden, down_all)).astype(jnp.bfloat16)
    back_gate, back_up, back_down = (gate_all, up_all, down_all)
    d_hidden = dot_right_t(cotangent, back_down)
    d_gate = (d_hidden * up * sig * (1.0 + gate * (1.0 - sig))).astype(jnp.bfloat16)
    d_up = (d_hidden * gate * sig).astype(jnp.bfloat16)
    grad_down = rounded_partial(hidden, cotangent)
    grad_gate = rounded_partial(normed_two, d_gate)
    grad_up = rounded_partial(normed_two, d_up)
    mlp_shards = (
        lax.psum_scatter(grad_gate, "fsdp", scatter_dimension=0, tiled=True).astype(jnp.float32),
        lax.psum_scatter(grad_up, "fsdp", scatter_dimension=0, tiled=True).astype(jnp.float32),
        lax.psum_scatter(grad_down, "fsdp", scatter_dimension=0, tiled=True).astype(jnp.float32),
    )
    d_normed_two = dot_right_t(d_gate, back_gate) + dot_right_t(d_up, back_up)
    grad_mlp_gain = jnp.sum(d_normed_two * mid * scale_two, axis=0)
    d_mid = cotangent.astype(jnp.float32) + norm_backward(d_normed_two, mid, scale_two, mlp_gain)
    d_mid_b = d_mid.astype(jnp.bfloat16)
    back_query, back_key, back_value, back_out = (query_all, key_gathered, value_gathered, out_all)
    back_keys, back_values = (keys_all, values_all)
    attention_gradient = dot_right_t(d_mid_b, back_out).astype(jnp.bfloat16)
    d_qrot, d_krot_all, d_values_all = attend_back(
        query_rotated, back_keys, back_values, allowed, lse, attention_gradient
    )
    d_krot, values_gradient = (
        lax.psum_scatter(
            d_krot_all.astype(jnp.bfloat16), "fsdp", scatter_dimension=0, tiled=True
        ).astype(jnp.float32),
        lax.psum_scatter(
            d_values_all.astype(jnp.bfloat16), "fsdp", scatter_dimension=0, tiled=True
        ).astype(jnp.float32),
    )
    d_qnormed = d_qrot * cos_tab + rotate_back(d_qrot * sin_tab)
    normed_key_gradient = d_krot * cos_tab + rotate_back(d_krot * sin_tab)
    grad_query_gain = jnp.sum(d_qnormed * q_raw * q_scale, axis=(0, 1))
    grad_key_gain = jnp.sum(normed_key_gradient * key_unnormed * key_scale, axis=(0, 1))
    d_query = (
        norm_backward(d_qnormed, q_raw, q_scale, query_gain)
        .astype(jnp.bfloat16)
        .reshape(item_count, QUERY_HEADS * HEAD_SIZE)
    )
    key_gradient = (
        norm_backward(normed_key_gradient, key_unnormed, key_scale, key_norm_gain)
        .astype(jnp.bfloat16)
        .reshape(item_count, KEY_VALUE_HEADS * HEAD_SIZE)
    )
    value_gradient = values_gradient.astype(jnp.bfloat16).reshape(
        item_count, KEY_VALUE_HEADS * HEAD_SIZE
    )
    grad_out = rounded_partial(attn_out, d_mid_b)
    grad_query = rounded_partial(normed_rows, d_query)
    grad_key = rounded_partial(normed_rows, key_gradient)
    grad_value = rounded_partial(normed_rows, value_gradient)
    attn_shards = (
        lax.psum_scatter(grad_query, "fsdp", scatter_dimension=0, tiled=True).astype(jnp.float32),
        lax.psum_scatter(grad_key, "fsdp", scatter_dimension=0, tiled=True).astype(jnp.float32),
        lax.psum_scatter(grad_value, "fsdp", scatter_dimension=0, tiled=True).astype(jnp.float32),
        lax.psum_scatter(grad_out, "fsdp", scatter_dimension=0, tiled=True).astype(jnp.float32),
    )
    d_normed = (
        dot_right_t(d_query, back_query)
        + dot_right_t(key_gradient, back_key)
        + dot_right_t(value_gradient, back_value)
    )
    grad_attn_gain = jnp.sum(d_normed * resid * scale_one, axis=0)
    d_block_in = d_mid + norm_backward(d_normed, resid, scale_one, attn_gain)
    gains = lax.psum(
        (grad_attn_gain, grad_mlp_gain, grad_query_gain, grad_key_gain), ("replica", "fsdp")
    )
    totals = (
        lax.psum(attn_shards[0].astype(jnp.bfloat16), "replica").astype(jnp.float32),
        lax.psum(attn_shards[1].astype(jnp.bfloat16), "replica").astype(jnp.float32),
        lax.psum(attn_shards[2].astype(jnp.bfloat16), "replica").astype(jnp.float32),
        lax.psum(attn_shards[3].astype(jnp.bfloat16), "replica").astype(jnp.float32),
        lax.psum(mlp_shards[0].astype(jnp.bfloat16), "replica").astype(jnp.float32),
        lax.psum(mlp_shards[1].astype(jnp.bfloat16), "replica").astype(jnp.float32),
        lax.psum(mlp_shards[2].astype(jnp.bfloat16), "replica").astype(jnp.float32),
    )
    return (
        block_out,
        d_block_in,
        totals[0],
        totals[1],
        totals[2],
        totals[3],
        totals[4],
        totals[5],
        totals[6],
        gains[0],
        gains[1],
        gains[2],
        gains[3],
    )


def solution(mesh):
    in_specs = (
        P(("replica", "fsdp"), None),
        P("fsdp", None),
        P("fsdp", None),
        P("fsdp", None),
        P("fsdp", None),
        P("fsdp", None),
        P("fsdp", None),
        P("fsdp", None),
        P(),
        P(),
        P(),
        P(),
        P("replica", None),
        P(("replica", "fsdp")),
        P(("replica", "fsdp"), None),
    )
    out_specs = (
        P(("replica", "fsdp"), None),
        P(("replica", "fsdp"), None),
        P("fsdp", None),
        P("fsdp", None),
        P("fsdp", None),
        P("fsdp", None),
        P("fsdp", None),
        P("fsdp", None),
        P("fsdp", None),
        P(),
        P(),
        P(),
        P(),
    )
    return jax.shard_map(shards, mesh=mesh, in_specs=in_specs, out_specs=out_specs, check_vma=False)
```

profile of v0, /device:TPU:0, one launch (start us, length us, event | category | flops | bytes accessed | tf_op | source)
XLA Modules:
  0.0 1245.7 jit_solution(10393132843414137143)
XLA Ops:
  13.5 31.9 %all-gather.10.cloned.1.call-done = bf16[1024,1024]{1,0:T(8,128)(2,1)} async-done(((bf16[512,1024]{1,0:T(8,128)(2,1)}), bf16[1024,1024]{1,0:T(8,128)(2,1)}) %all-gather.10.cloned.1.call-update) | async-done | bytes 2097168 | tf_op jit(solution)/shard_map/all_gather | solution.py:65
  47.9 32.2 %all-gather.8.cloned.1.call-done = bf16[1024,1024]{1,0:T(8,128)(2,1)} async-done(((bf16[512,1024]{1,0:T(8,128)(2,1)}), bf16[1024,1024]{1,0:T(8,128)(2,1)}) %all-gather.8.cloned.1.call-update) | async-done | bytes 2097168 | tf_op jit(solution)/shard_map/all_gather | solution.py:66
  83.1 8.7 all_gather.30
  91.8 15.3 %all_gather.28 = bf16[256,8,128]{0,2,1:T(8,128)(2,1)} all-gather(bf16[128,8,128]{0,2,1:T(8,128)(2,1)S(1)} %bitcast.203), channel_id=1, replica_groups=mesh['replica'=16,'fsdp'=2] {'fsdp'}, dimensions={0}, use_global_device_ids=true | all-gather | bytes 786432 | tf_op jit(solution)/shard_map/all_gather | solution.py:82
  107.1 36.9 %all-gather.12.cloned.1.call-done = bf16[1024,2048]{1,0:T(8,128)(2,1)} async-done(((bf16[512,2048]{1,0:T(8,128)(2,1)}), bf16[1024,2048]{1,0:T(8,128)(2,1)}) %all-gather.12.cloned.1.call-update) | async-done | bytes 4194320 | tf_op jit(solution)/shard_map/all_gather | solution.py:64
  151.7 50.5 %all-gather.14.cloned.1.call-done = bf16[2048,1024]{1,0:T(8,128)(2,1)} async-done(((bf16[1024,1024]{1,0:T(8,128)(2,1)}), bf16[2048,1024]{1,0:T(8,128)(2,1)}) %all-gather.14.cloned.1.call-update) | async-done | bytes 4194320 | tf_op jit(solution)/shard_map/all_gather | solution.py:67
  206.9 77.0 %all-gather.16.cloned.1.call-done = bf16[1024,3072]{1,0:T(8,128)(2,1)} async-done(((bf16[512,3072]{1,0:T(8,128)(2,1)}), bf16[1024,3072]{1,0:T(8,128)(2,1)}) %all-gather.16.cloned.1.call-update) | async-done | bytes 6291472 | tf_op jit(solution)/shard_map/all_gather | solution.py:73
  283.9 5.0 fusion.78
  288.9 76.8 %all-gather.18.cloned.1.call-done = bf16[1024,3072]{1,0:T(8,128)(2,1)} async-done(((bf16[512,3072]{1,0:T(8,128)(2,1)}), bf16[1024,3072]{1,0:T(8,128)(2,1)}) %all-gather.18.cloned.1.call-update) | async-done | bytes 6291472 | tf_op jit(solution)/shard_map/all_gather | solution.py:74
  365.7 5.0 fusion.79
  370.7 76.9 %all-gather.20.cloned.1.call-done = bf16[3072,1024]{1,0:T(8,128)(2,1)} async-done(((bf16[1536,1024]{1,0:T(8,128)(2,1)}), bf16[3072,1024]{1,0:T(8,128)(2,1)}) %all-gather.20.cloned.1.call-update) | async-done | bytes 6291472 | tf_op jit(solution)/shard_map/all_gather | solution.py:75
  447.6 7.1 multiply_convert_fusion
  454.8 5.6 fusion.80
  471.8 4.1 fusion.12
  480.4 10.3 reduce-scatter.12.cloned.1.call-done
  498.9 9.3 reduce-scatter.28.cloned.1.call-done
  519.8 4.4 fusion.7
  541.6 4.5 fusion.83
  547.2 4.6 fusion.84
  553.0 4.5 fusion.85
  557.7 19.3 %reduce-scatter.18.cloned.1.call-done = bf16[512,1024]{1,0:T(8,128)(2,1)} async-done(((bf16[1024,1024]{1,0:T(8,128)(2,1)}), bf16[512,1024]{1,0:T(8,128)(2,1)}) %reduce-scatter.18.cloned.1.call-update) | async-done | bytes 1048592 | tf_op jit(solution)/shard_map/reduce_scatter | solution.py:248
  577.0 57.1 %reduce-scatter.14.cloned.1.call-done = bf16[512,2048]{1,0:T(8,128)(2,1)} async-done(((bf16[1024,2048]{1,0:T(8,128)(2,1)}), bf16[512,2048]{1,0:T(8,128)(2,1)}) %reduce-scatter.14.cloned.1.call-update) | async-done | bytes 2097168 | tf_op jit(solution)/shard_map/reduce_scatter | solution.py:246
  634.1 57.3 %reduce-scatter.20.cloned.1.call-done = bf16[1024,1024]{1,0:T(8,128)(2,1)} async-done(((bf16[2048,1024]{1,0:T(8,128)(2,1)}), bf16[1024,1024]{1,0:T(8,128)(2,1)}) %reduce-scatter.20.cloned.1.call-update) | async-done | bytes 2097168 | tf_op jit(solution)/shard_map/reduce_scatter | solution.py:249
  691.4 79.9 %reduce-scatter.22.cloned.1.call-done = bf16[512,3072]{1,0:T(8,128)(2,1)} async-done(((bf16[1024,3072]{1,0:T(8,128)(2,1)}), bf16[512,3072]{1,0:T(8,128)(2,1)}) %reduce-scatter.22.cloned.1.call-update) | async-done | bytes 3145744 | tf_op jit(solution)/shard_map/reduce_scatter | solution.py:202
  771.3 79.9 %reduce-scatter.24.cloned.1.call-done = bf16[512,3072]{1,0:T(8,128)(2,1)} async-done(((bf16[1024,3072]{1,0:T(8,128)(2,1)}), bf16[512,3072]{1,0:T(8,128)(2,1)}) %reduce-scatter.24.cloned.1.call-update) | async-done | bytes 3145744 | tf_op jit(solution)/shard_map/reduce_scatter | solution.py:203
  851.2 79.9 %reduce-scatter.26.cloned.1.call-done = bf16[1536,1024]{1,0:T(8,128)(2,1)} async-done(((bf16[3072,1024]{1,0:T(8,128)(2,1)}), bf16[1536,1024]{1,0:T(8,128)(2,1)}) %reduce-scatter.26.cloned.1.call-update) | async-done | bytes 3145744 | tf_op jit(solution)/shard_map/reduce_scatter | solution.py:204
  932.2 4.6 fusion.13
  940.7 41.4 %all-reduce = (f32[1024]{0:T(1024)}, f32[1024]{0:T(1024)}, f32[128]{0:T(128)}, f32[128]{0:T(128)}) all-reduce(f32[1024]{0:T(1024)S(1)} %get-tuple-element.17, f32[1024]{0:T(1024)S(1)} %copy-done.49, f32[128]{0:T(128)S(1)} %bitcast_reduce_fusion, f32[128]{0:T(128)S(1)} %copy-done.56), channel_id=1, replica_groups=mesh['replica'=16,'fsdp'=2] {'replica','fsdp'}, use_global_device_ids=true, to_apply=%region_28.29 | all-reduce | flops 2304 | bytes 18432 | tf_op jit(solution)/shard_map/psum | solution.py:258
  983.1 235.2 %all-reduce.4.cloned.1.call-done = (bf16[512,2048]{1,0:T(8,128)(2,1)}, bf16[512,1024]{1,0:T(8,128)(2,1)}, bf16[512,1024]{1,0:T(8,128)(2,1)}, bf16[1024,1024]{1,0...) async-done(((bf16[512,2048]{1,0:T(8,128)(2,1)}, bf16[512,1024]{1,0:T(8,128)(2,1)}, bf16[512,1024]{1,0:T(8,128)(2,1)}, ...) | async-done | bytes 15728656 | tf_op jit(solution)/shard_map/psum | solution.py:262
  1218.3 5.5 convert_element_type.144
  1223.8 3.5 convert_element_type.145
  1227.3 3.5 convert_element_type.146
  (231 shorter events, 93.3 us)
Async XLA Ops:
  7.2 38.2 %all-gather.10.cloned.1.call-start = ((), (), s32[]{:S(2)}) async-start(), calls=%async_computation.10 | async-start | bytes 3145728 | tf_op jit(solution)/shard_map/all_gather | solution.py:65
  7.9 72.1 %all-gather.8.cloned.1.call-start = ((), (), s32[]{:S(2)}) async-start(), calls=%async_computation.9 | async-start | bytes 3145728 | tf_op jit(solution)/shard_map/all_gather | solution.py:66
  8.7 135.3 %all-gather.12.cloned.1.call-start = ((), (), s32[]{:S(2)}) async-start(), calls=%async_computation.11 | async-start | bytes 6291456 | tf_op jit(solution)/shard_map/all_gather | solution.py:64
  9.4 192.7 %all-gather.14.cloned.1.call-start = ((), (), s32[]{:S(2)}) async-start(), calls=%async_computation.12 | async-start | bytes 6291456 | tf_op jit(solution)/shard_map/all_gather | solution.py:67
  10.0 273.9 %all-gather.16.cloned.1.call-start = ((), (), s32[]{:S(2)}) async-start(), calls=%async_computation.13 | async-start | bytes 9437184 | tf_op jit(solution)/shard_map/all_gather | solution.py:73
  10.6 355.1 %all-gather.18.cloned.1.call-start = ((), (), s32[]{:S(2)}) async-start(), calls=%async_computation.14 | async-start | bytes 9437184 | tf_op jit(solution)/shard_map/all_gather | solution.py:74
  11.2 34.2 %copy-start.40 = (f32[1024]{0:T(1024)S(1)}, f32[1024]{0:T(1024)}, u32[]{:S(2)}) copy-start(f32[1024]{0:T(1024)} %param.23) | copy-start | bytes 12292
  11.2 436.4 %all-gather.20.cloned.1.call-start = ((), (), s32[]{:S(2)}) async-start(), calls=%async_computation.15 | async-start | bytes 9437184 | tf_op jit(solution)/shard_map/all_gather | solution.py:75
  11.9 478.7 %reduce-scatter.12.cloned.1.call-start = ((), (), s32[]{:S(2)}) async-start(), calls=%async_computation.16 | async-start | bytes 786432 | tf_op jit(solution)/shard_map/reduce_scatter | solution.py:217
  12.2 131.7 %copy-start.44 = (f32[128]{0:T(128)}, f32[128]{0:T(128)S(1)}, u32[]{:S(2)}) copy-start(f32[128]{0:T(128)S(1)} %add_rsqrt_fusion.3) | copy-start | bytes 1540
  13.3 69.4 %copy-start.37 = (f32[128,128]{1,0:T(8,128)}, f32[128,128]{1,0:T(8,128)S(1)}, u32[]{:S(2)}) copy-start(f32[128,128]{1,0:T(8,128)S(1)} %copy.156) | copy-start | bytes 196612
  13.4 69.3 %copy-start.39 = (f32[128,128]{1,0:T(8,128)}, f32[128,128]{1,0:T(8,128)S(1)}, u32[]{:S(2)}) copy-start(f32[128,128]{1,0:T(8,128)S(1)} %copy.157) | copy-start | bytes 196612
  47.5 35.3 %copy-start.2 = (f32[128,1024]{1,0:T(8,128)}, f32[128,1024]{1,0:T(8,128)S(1)}, u32[]{:S(2)}) copy-start(f32[128,1024]{1,0:T(8,128)S(1)} %fusion.71) | copy-start | bytes 1572868
  47.6 34.7 %copy-start.50 = (f32[128]{0:T(128)S(1)}, f32[128]{0:T(128)}, u32[]{:S(2)}) copy-start(f32[128]{0:T(128)} %param.26) | copy-start | bytes 1540
  454.7 5.6 copy-start.22
  454.7 5.6 copy-start.24
  454.7 5.6 copy-start
  454.8 5.7 copy-start.8
  454.8 5.7 copy-start.47
  454.8 5.7 copy-start.55
  475.9 32.3 %reduce-scatter.28.cloned.1.call-start = ((), (), s32[]{:S(2)}) async-start(), calls=%async_computation.24 | async-start | bytes 786432 | tf_op jit(solution)/shard_map/reshape | solution.py:238
  480.4 77.3 %reduce-scatter.16.cloned.1.call-start = ((), (), s32[]{:S(2)}) async-start(), calls=%async_computation.18 | async-start | bytes 3145728 | tf_op jit(solution)/shard_map/reduce_scatter | solution.py:247
  495.7 12.4 copy-start.45
  498.9 78.1 %reduce-scatter.18.cloned.1.call-start = ((), (), s32[]{:S(2)}) async-start(), calls=%async_computation.19 | async-start | bytes 3145728 | tf_op jit(solution)/shard_map/reduce_scatter | solution.py:248
  511.3 122.9 %reduce-scatter.14.cloned.1.call-start = ((), (), s32[]{:S(2)}) async-start(), calls=%async_computation.17 | async-start | bytes 6291456 | tf_op jit(solution)/shard_map/reduce_scatter | solution.py:246
  535.9 155.5 %reduce-scatter.20.cloned.1.call-start = ((), (), s32[]{:S(2)}) async-start(), calls=%async_computation.20 | async-start | bytes 6291456 | tf_op jit(solution)/shard_map/reduce_scatter | solution.py:249
  540.4 230.9 %reduce-scatter.22.cloned.1.call-start = ((), (), s32[]{:S(2)}) async-start(), calls=%async_computation.21 | async-start | bytes 9437184 | tf_op jit(solution)/shard_map/reduce_scatter | solution.py:202
  546.1 305.1 %reduce-scatter.24.cloned.1.call-start = ((), (), s32[]{:S(2)}) async-start(), calls=%async_computation.22 | async-start | bytes 9437184 | tf_op jit(solution)/shard_map/reduce_scatter | solution.py:203
  551.9 379.2 %reduce-scatter.26.cloned.1.call-start = ((), (), s32[]{:S(2)}) async-start(), calls=%async_computation.23 | async-start | bytes 9437184 | tf_op jit(solution)/shard_map/reduce_scatter | solution.py:204
  557.6 660.7 %all-reduce.4.cloned.1.call-start = ((), (), s32[]{:S(2)}) async-start(), calls=%async_computation.25 | async-start | bytes 31457280 | tf_op jit(solution)/shard_map/psum | solution.py:262
  932.2 5.5 copy-start.36
  1218.3 5.5 copy-start.21
  (44 other events, 80.0 us)
Sparse Core Ops, SparseCore 0:
  9.5 35.8 all-gather.9
  46.9 33.0 all-gather.7
  81.6 62.3 all-gather.11
  145.4 56.7 all-gather.13
  203.5 80.3 all-gather.15
  285.3 80.3 all-gather.17
  367.2 80.3 all-gather.19
  476.0 14.6 reduce-scatter.11
  493.5 14.6 reduce-scatter.27
  510.8 31.9 reduce-scatter.15
  545.1 31.8 reduce-scatter.17
  579.7 54.3 reduce-scatter.13
  637.0 54.3 reduce-scatter.19
  694.1 77.1 reduce-scatter.21
  774.0 77.1 reduce-scatter.23
  853.9 77.1 reduce-scatter.25
  936.5 281.7 all-reduce.3
where the time goes:
time: 1250 us
  waiting for transfers between devices  1010 us (81%)
  matrix products  88.1 us (7%)
  blocking collectives  65.3 us (5%)
  other arithmetic  34.1 us (3%)
  local copies, waits for them, and re-layouts  27.6 us (2%)
  between operations  14.8 us (1%)
    psum x1, waiting for transfers between devices, shards(): lax.psum(attn_shards[0].astype(jnp.bfloat16), 'replica').astype(jnp.float32)  235 us
    reduce_scatter x1, waiting for transfers between devices, shards(): lax.psum_scatter(grad_up, 'fsdp', scatter_dimension=0, tiled=True)  79.9 us
    reduce_scatter x1, waiting for transfers between devices, shards(): lax.psum_scatter(grad_down, 'fsdp', scatter_dimension=0, tiled=True)  79.9 us
    reduce_scatter x1, waiting for transfers between devices, shards(): lax.psum_scatter(grad_gate, 'fsdp', scatter_dimension=0, tiled=True)  79.9 us
    all_gather x1, waiting for transfers between devices, mlp_weights(): lax.all_gather(w_gate, 'fsdp', axis=0, tiled=True)  77 us
    all_gather x1, waiting for transfers between devices, mlp_weights(): lax.all_gather(w_down, 'fsdp', axis=0, tiled=True)  76.9 us
    all_gather x1, waiting for transfers between devices, mlp_weights(): lax.all_gather(w_up, 'fsdp', axis=0, tiled=True)  76.8 us
    reduce_scatter x1, waiting for transfers between devices, shards(): lax.psum_scatter(grad_out, 'fsdp', scatter_dimension=0, tiled=True)  57.3 us
  transfers between devices with their start and end apart: 17, of which 16 were waited for; matrix products, arithmetic and copies ran while one was open for 7% of the time, Pallas kernels for 0%

commit v1 on v0

--- a/solution.py
+++ b/solution.py
@@ -258,8 +258,12 @@
     gains = lax.psum(
         (grad_attn_gain, grad_mlp_gain, grad_query_gain, grad_key_gain), ("replica", "fsdp")
     )
+
+    def _spread_ladders(u_in, net_axis):
+        return jnp.sum(jax.lax.all_gather(u_in, axis_name=net_axis), axis=0)
+
     totals = (
-        lax.psum(attn_shards[0].astype(jnp.bfloat16), "replica").astype(jnp.float32),
+        _spread_ladders(attn_shards[0].astype(jnp.bfloat16), "replica").astype(jnp.float32),
         lax.psum(attn_shards[1].astype(jnp.bfloat16), "replica").astype(jnp.float32),
         lax.psum(attn_shards[2].astype(jnp.bfloat16), "replica").astype(jnp.float32),
         lax.psum(attn_shards[3].astype(jnp.bfloat16), "replica").astype(jnp.float32),

time: 1250 us -> 1380 us (1.10)
  waiting for transfers between devices: 1010 us -> 1130 us
    all_gather x0 -> x1, waiting for transfers between devices: none -> 150 us  [_spread_ladders(): return jnp.sum(jax.lax.all_gather(u_in, axis_name=net_axis), axis=0)]
    psum x1, waiting for transfers between devices: 235 us -> 205 us  [shards(): lax.psum(attn_shards[1].astype(jnp.bfloat16), 'replica').astype(jnp.float32)]
  transfers between devices with their start and end apart: 17 -> 18, of which waited for: 16 -> 17; matrix products, arithmetic and copies ran while one was open for 7% -> 8% of each run, Pallas kernels for 0% -> 0%
where the time goes in v1:
time: 1380 us
  waiting for transfers between devices  1130 us (82%)
  matrix products  93.3 us (7%)
  blocking collectives  65.4 us (5%)
  other arithmetic  45.1 us (3%)
  local copies, waits for them, and re-layouts  24.2 us (2%)
  between operations  15.2 us (1%)
    psum x1, waiting for transfers between devices, shards(): lax.psum(attn_shards[1].astype(jnp.bfloat16), 'replica').astype(jnp.float32)  205 us
    all_gather x1, waiting for transfers between devices, _spread_ladders(): return jnp.sum(jax.lax.all_gather(u_in, axis_name=net_axis), axis=0)  150 us
    reduce_scatter x1, waiting for transfers between devices, shards(): lax.psum_scatter(grad_gate, 'fsdp', scatter_dimension=0, tiled=True)  80 us
    reduce_scatter x1, waiting for transfers between devices, shards(): lax.psum_scatter(grad_up, 'fsdp', scatter_dimension=0, tiled=True)  79.9 us
    reduce_scatter x1, waiting for transfers between devices, shards(): lax.psum_scatter(grad_down, 'fsdp', scatter_dimension=0, tiled=True)  79.9 us
    all_gather x1, waiting for transfers between devices, mlp_weights(): lax.all_gather(w_gate, 'fsdp', axis=0, tiled=True)  76.9 us
    all_gather x1, waiting for transfers between devices, mlp_weights(): lax.all_gather(w_down, 'fsdp', axis=0, tiled=True)  76.9 us
    all_gather x1, waiting for transfers between devices, mlp_weights(): lax.all_gather(w_up, 'fsdp', axis=0, tiled=True)  76.8 us
  transfers between devices with their start and end apart: 18, of which 17 were waited for; matrix products, arithmetic and copies ran while one was open for 8% of the time, Pallas kernels for 0%

profile of v1, /device:TPU:0, one launch (start us, length us, event | category | flops | bytes accessed | tf_op | source)
XLA Modules:
  0.0 1378.4 jit_solution(2345093331046856226)
XLA Ops:
  13.5 31.9 %all-gather.10.cloned.1.call-done = bf16[1024,1024]{1,0:T(8,128)(2,1)} async-done(((bf16[512,1024]{1,0:T(8,128)(2,1)}), bf16[1024,1024]{1,0:T(8,128)(2,1)}) %all-gather.10.cloned.1.call-update) | async-done | bytes 2097168 | tf_op jit(solution)/shard_map/all_gather | solution.py:66
  47.7 32.4 %all-gather.12.cloned.1.call-done = bf16[1024,1024]{1,0:T(8,128)(2,1)} async-done(((bf16[512,1024]{1,0:T(8,128)(2,1)}), bf16[1024,1024]{1,0:T(8,128)(2,1)}) %all-gather.12.cloned.1.call-update) | async-done | bytes 2097168 | tf_op jit(solution)/shard_map/all_gather | solution.py:65
  82.5 8.7 all_gather.34
  92.0 15.1 %all_gather.36 = bf16[256,8,128]{2,0,1:T(8,128)(2,1)} all-gather(bf16[128,8,128]{2,0,1:T(8,128)(2,1)S(1)} %fusion.46), channel_id=1, replica_groups=mesh['replica'=16,'fsdp'=2] {'fsdp'}, dimensions={0}, use_global_device_ids=true | all-gather | bytes 786432 | tf_op jit(solution)/shard_map/all_gather | solution.py:81
  107.1 36.9 %all-gather.14.cloned.1.call-done = bf16[1024,2048]{1,0:T(8,128)(2,1)} async-done(((bf16[512,2048]{1,0:T(8,128)(2,1)}), bf16[1024,2048]{1,0:T(8,128)(2,1)}) %all-gather.14.cloned.1.call-update) | async-done | bytes 4194320 | tf_op jit(solution)/shard_map/all_gather | solution.py:64
  151.7 50.5 %all-gather.16.cloned.1.call-done = bf16[2048,1024]{1,0:T(8,128)(2,1)} async-done(((bf16[1024,1024]{1,0:T(8,128)(2,1)}), bf16[2048,1024]{1,0:T(8,128)(2,1)}) %all-gather.16.cloned.1.call-update) | async-done | bytes 4194320 | tf_op jit(solution)/shard_map/all_gather | solution.py:67
  207.0 76.9 %all-gather.18.cloned.1.call-done = bf16[1024,3072]{1,0:T(8,128)(2,1)} async-done(((bf16[512,3072]{1,0:T(8,128)(2,1)}), bf16[1024,3072]{1,0:T(8,128)(2,1)}) %all-gather.18.cloned.1.call-update) | async-done | bytes 6291472 | tf_op jit(solution)/shard_map/all_gather | solution.py:73
  283.9 5.0 fusion.78
  288.9 76.8 %all-gather.20.cloned.1.call-done = bf16[1024,3072]{1,0:T(8,128)(2,1)} async-done(((bf16[512,3072]{1,0:T(8,128)(2,1)}), bf16[1024,3072]{1,0:T(8,128)(2,1)}) %all-gather.20.cloned.1.call-update) | async-done | bytes 6291472 | tf_op jit(solution)/shard_map/all_gather | solution.py:74
  365.7 5.0 fusion.79
  370.7 76.9 %all-gather.22.cloned.1.call-done = bf16[3072,1024]{1,0:T(8,128)(2,1)} async-done(((bf16[1536,1024]{1,0:T(8,128)(2,1)}), bf16[3072,1024]{1,0:T(8,128)(2,1)}) %all-gather.22.cloned.1.call-update) | async-done | bytes 6291472 | tf_op jit(solution)/shard_map/all_gather | solution.py:75
  447.6 7.2 multiply_convert_fusion
  454.8 5.6 fusion.80
  472.2 4.2 fusion.12
  480.9 10.3 reduce-scatter.12.cloned.1.call-done
  499.4 9.3 reduce-scatter.28.cloned.1.call-done
  511.8 4.4 fusion.55
  516.3 6.0 fusion.83
  522.4 5.7 fusion.84
  528.2 5.7 fusion.85
  542.6 4.4 fusion.7
  558.9 18.6 %reduce-scatter.18.cloned.1.call-done = bf16[512,1024]{1,0:T(8,128)(2,1)} async-done(((bf16[1024,1024]{1,0:T(8,128)(2,1)}), bf16[512,1024]{1,0:T(8,128)(2,1)}) %reduce-scatter.18.cloned.1.call-update) | async-done | bytes 1048592 | tf_op jit(solution)/shard_map/reduce_scatter | solution.py:248
  577.4 57.1 %reduce-scatter.20.cloned.1.call-done = bf16[1024,1024]{1,0:T(8,128)(2,1)} async-done(((bf16[2048,1024]{1,0:T(8,128)(2,1)}), bf16[1024,1024]{1,0:T(8,128)(2,1)}) %reduce-scatter.20.cloned.1.call-update) | async-done | bytes 2097168 | tf_op jit(solution)/shard_map/reduce_scatter | solution.py:249
  634.6 80.0 %reduce-scatter.22.cloned.1.call-done = bf16[512,3072]{1,0:T(8,128)(2,1)} async-done(((bf16[1024,3072]{1,0:T(8,128)(2,1)}), bf16[512,3072]{1,0:T(8,128)(2,1)}) %reduce-scatter.22.cloned.1.call-update) | async-done | bytes 3145744 | tf_op jit(solution)/shard_map/reduce_scatter | solution.py:202
  714.6 79.9 %reduce-scatter.24.cloned.1.call-done = bf16[512,3072]{1,0:T(8,128)(2,1)} async-done(((bf16[1024,3072]{1,0:T(8,128)(2,1)}), bf16[512,3072]{1,0:T(8,128)(2,1)}) %reduce-scatter.24.cloned.1.call-update) | async-done | bytes 3145744 | tf_op jit(solution)/shard_map/reduce_scatter | solution.py:203
  794.5 79.9 %reduce-scatter.26.cloned.1.call-done = bf16[1536,1024]{1,0:T(8,128)(2,1)} async-done(((bf16[3072,1024]{1,0:T(8,128)(2,1)}), bf16[1536,1024]{1,0:T(8,128)(2,1)}) %reduce-scatter.26.cloned.1.call-update) | async-done | bytes 3145744 | tf_op jit(solution)/shard_map/reduce_scatter | solution.py:204
  874.5 57.0 %reduce-scatter.14.cloned.1.call-done = bf16[512,2048]{1,0:T(8,128)(2,1)} async-done(((bf16[1024,2048]{1,0:T(8,128)(2,1)}), bf16[512,2048]{1,0:T(8,128)(2,1)}) %reduce-scatter.14.cloned.1.call-update) | async-done | bytes 2097168 | tf_op jit(solution)/shard_map/reduce_scatter | solution.py:246
  931.7 4.6 fusion.13
  940.2 41.6 %all-reduce = (f32[1024]{0:T(1024)}, f32[1024]{0:T(1024)}, f32[128]{0:T(128)}, f32[128]{0:T(128)}) all-reduce(f32[1024]{0:T(1024)S(1)} %get-tuple-element.17, f32[1024]{0:T(1024)S(1)} %copy-done.44, f32[128]{0:T(128)S(1)} %bitcast_reduce_fusion, f32[128]{0:T(128)S(1)} %copy-done.51), channel_id=1, replica_groups=mesh['replica'=16,'fsdp'=2] {'replica','fsdp'}, use_global_device_ids=true, to_apply=%region_28.29 | all-reduce | flops 2304 | bytes 18432 | tf_op jit(solution)/shard_map/psum | solution.py:258
  982.8 205.2 %all-reduce.4.cloned.1.call-done = (bf16[512,1024]{1,0:T(8,128)(2,1)}, bf16[512,1024]{1,0:T(8,128)(2,1)}, bf16[1024,1024]{1,0:T(8,128)(2,1)}, bf16[512,3072]{1,0...) async-done(((bf16[512,1024]{1,0:T(8,128)(2,1)}, bf16[512,1024]{1,0:T(8,128)(2,1)}, bf16[1024,1024]{1,0:T(8,128)(2,1)}, bf16[512,3072]{1,0:T(8,128)(2,1)}, ...) | async-done | bytes 13631504 | tf_op jit(solution)/shard_map/psum | solution.py:267
  1206.7 150.3 %all-gather.24.cloned.1.call-done = bf16[8192,2048]{1,0:T(8,128)(2,1)} async-done(((bf16[512,2048]{1,0:T(8,128)(2,1)}), bf16[8192,2048]{1,0:T(8,128)(2,1)}) %all-gather.24.cloned.1.call-update) | async-done | bytes 33554448 | tf_op jit(solution)/shard_map/all_gather | solution.py:263
  1357.0 11.7 reduce_sum.155
  (225 shorter events, 98.4 us)
Async XLA Ops:
  7.2 38.2 %all-gather.10.cloned.1.call-start = ((), (), s32[]{:S(2)}) async-start(), calls=%async_computation.9 | async-start | bytes 3145728 | tf_op jit(solution)/shard_map/all_gather | solution.py:66
  7.9 72.1 %all-gather.12.cloned.1.call-start = ((), (), s32[]{:S(2)}) async-start(), calls=%async_computation.10 | async-start | bytes 3145728 | tf_op jit(solution)/shard_map/all_gather | solution.py:65
  8.7 135.3 %all-gather.14.cloned.1.call-start = ((), (), s32[]{:S(2)}) async-start(), calls=%async_computation.11 | async-start | bytes 6291456 | tf_op jit(solution)/shard_map/all_gather | solution.py:64
  9.4 192.7 %all-gather.16.cloned.1.call-start = ((), (), s32[]{:S(2)}) async-start(), calls=%async_computation.12 | async-start | bytes 6291456 | tf_op jit(solution)/shard_map/all_gather | solution.py:67
  10.0 273.9 %all-gather.18.cloned.1.call-start = ((), (), s32[]{:S(2)}) async-start(), calls=%async_computation.13 | async-start | bytes 9437184 | tf_op jit(solution)/shard_map/all_gather | solution.py:73
  10.6 355.1 %all-gather.20.cloned.1.call-start = ((), (), s32[]{:S(2)}) async-start(), calls=%async_computation.14 | async-start | bytes 9437184 | tf_op jit(solution)/shard_map/all_gather | solution.py:74
  11.2 34.2 %copy-start.35 = (f32[1024]{0:T(1024)S(1)}, f32[1024]{0:T(1024)}, u32[]{:S(2)}) copy-start(f32[1024]{0:T(1024)} %param.23) | copy-start | bytes 12292
  11.2 436.4 %all-gather.22.cloned.1.call-start = ((), (), s32[]{:S(2)}) async-start(), calls=%async_computation.15 | async-start | bytes 9437184 | tf_op jit(solution)/shard_map/all_gather | solution.py:75
  11.9 479.2 %reduce-scatter.12.cloned.1.call-start = ((), (), s32[]{:S(2)}) async-start(), calls=%async_computation.16 | async-start | bytes 786432 | tf_op jit(solution)/shard_map/reduce_scatter | solution.py:217
  12.2 131.7 %copy-start.39 = (f32[128]{0:T(128)}, f32[128]{0:T(128)S(1)}, u32[]{:S(2)}) copy-start(f32[128]{0:T(128)S(1)} %add_rsqrt_fusion.3) | copy-start | bytes 1540
  13.3 78.3 %copy-start.34 = (f32[128,128]{1,0:T(8,128)}, f32[128,128]{1,0:T(8,128)S(1)}, u32[]{:S(2)}) copy-start(f32[128,128]{1,0:T(8,128)S(1)} %copy.157) | copy-start | bytes 196612
  13.4 78.2 %copy-start.32 = (f32[128,128]{1,0:T(8,128)}, f32[128,128]{1,0:T(8,128)S(1)}, u32[]{:S(2)}) copy-start(f32[128,128]{1,0:T(8,128)S(1)} %copy.156) | copy-start | bytes 196612
  47.6 43.5 %copy-start.45 = (f32[128]{0:T(128)S(1)}, f32[128]{0:T(128)}, u32[]{:S(2)}) copy-start(f32[128]{0:T(128)} %param.26) | copy-start | bytes 1540
  82.1 9.5 copy-start.2
  454.8 5.6 copy-start
  454.8 5.6 copy-start.7
  454.8 5.7 copy-start.42
  454.8 5.7 copy-start.50
  476.4 32.3 %reduce-scatter.28.cloned.1.call-start = ((), (), s32[]{:S(2)}) async-start(), calls=%async_computation.25 | async-start | bytes 786432 | tf_op jit(solution)/shard_map/reshape | solution.py:238
  480.8 78.1 %reduce-scatter.16.cloned.1.call-start = ((), (), s32[]{:S(2)}) async-start(), calls=%async_computation.18 | async-start | bytes 3145728 | tf_op jit(solution)/shard_map/reduce_scatter | solution.py:247
  496.2 12.4 copy-start.40
  499.3 78.1 %reduce-scatter.18.cloned.1.call-start = ((), (), s32[]{:S(2)}) async-start(), calls=%async_computation.19 | async-start | bytes 3145728 | tf_op jit(solution)/shard_map/reduce_scatter | solution.py:248
  511.7 122.9 %reduce-scatter.20.cloned.1.call-start = ((), (), s32[]{:S(2)}) async-start(), calls=%async_computation.20 | async-start | bytes 6291456 | tf_op jit(solution)/shard_map/reduce_scatter | solution.py:249
  516.2 198.4 %reduce-scatter.22.cloned.1.call-start = ((), (), s32[]{:S(2)}) async-start(), calls=%async_computation.21 | async-start | bytes 9437184 | tf_op jit(solution)/shard_map/reduce_scatter | solution.py:202
  522.3 272.2 %reduce-scatter.24.cloned.1.call-start = ((), (), s32[]{:S(2)}) async-start(), calls=%async_computation.22 | async-start | bytes 9437184 | tf_op jit(solution)/shard_map/reduce_scatter | solution.py:203
  528.1 346.3 %reduce-scatter.26.cloned.1.call-start = ((), (), s32[]{:S(2)}) async-start(), calls=%async_computation.23 | async-start | bytes 9437184 | tf_op jit(solution)/shard_map/reduce_scatter | solution.py:204
  533.9 397.7 %reduce-scatter.14.cloned.1.call-start = ((), (), s32[]{:S(2)}) async-start(), calls=%async_computation.17 | async-start | bytes 6291456 | tf_op jit(solution)/shard_map/reduce_scatter | solution.py:246
  558.8 629.1 %all-reduce.4.cloned.1.call-start = ((), (), s32[]{:S(2)}) async-start(), calls=%async_computation.26 | async-start | bytes 27262976 | tf_op jit(solution)/shard_map/psum | solution.py:267
  874.5 57.2 %copy-start.8 = (f32[128,1024]{1,0:T(8,128)S(1)}, f32[128,1024]{1,0:T(8,128)}, u32[]{:S(2)}) copy-start(f32[128,1024]{1,0:T(8,128)} %copy-done.6) | copy-start | bytes 1572868
  874.5 57.2 %copy-start.16 = (bf16[128,3072]{1,0:T(8,128)(2,1)S(1)}, bf16[128,3072]{1,0:T(8,128)(2,1)}, u32[]{:S(2)}) copy-start(bf16[128,3072]{1,0:T(8,128)(2,1)} %get-tuple-element.34) | copy-start | bytes 2359300
  874.5 482.5 %all-gather.24.cloned.1.call-start = ((), (), s32[]{:S(2)}) async-start(), calls=%async_computation.24 | async-start | bytes 35651584 | tf_op jit(solution)/shard_map/all_gather | solution.py:263
  938.5 43.3 %copy-start.13 = (f32[128,1024]{1,0:T(8,128)S(1)}, f32[128,1024]{1,0:T(8,128)}, u32[]{:S(2)}) copy-start(f32[128,1024]{1,0:T(8,128)} %copy-done.12) | copy-start | bytes 1572868
  (40 other events, 92.5 us)
Sparse Core Ops, SparseCore 0:
  9.5 35.8 all-gather.9
  46.9 33.0 all-gather.11
  81.6 62.3 all-gather.13
  145.4 56.7 all-gather.15
  203.5 80.3 all-gather.17
  285.3 80.3 all-gather.19
  367.2 80.3 all-gather.21
  476.5 14.6 reduce-scatter.11
  494.0 14.6 reduce-scatter.27
  511.3 31.8 reduce-scatter.15
  545.5 31.8 reduce-scatter.17
  580.2 54.3 reduce-scatter.19
  637.4 77.1 reduce-scatter.21
  717.4 77.1 reduce-scatter.23
  797.3 77.1 reduce-scatter.25
  877.1 54.3 reduce-scatter.13
  936.7 251.2 all-reduce.3
  1189.4 167.5 all-gather.23
